TPU v7x, 32 devices: a whole 2x2x4 slice. The times are simulated.
32 devices in a mesh: blk: 8 (over z, x), road: 4 (over y, core).
Axes of the slice: x: 2, y: 2, z: 4, core: 2. Of those that a mesh axis runs over, the one named last changes fastest.
Arguments:
- disp: float32 [3, 16, 64, 1024], P(None, None, 'road', 'blk'), may hold values from -1.2 to 1.2
- veloc: float32 [3, 16, 64, 1024], P(None, None, 'road', 'blk'), may hold values from -6 to 6
- stiff: float32 [3, 16, 64, 1024], P(None, None, 'road', 'blk'), may hold values from 0.5 to 2
- mass: float32 [16, 64, 1024], P(None, 'road', 'blk'), may hold values from 1 to 4
- road_height: float32 [16384], P('road'), may hold values from -1.2 to 1.2
- road_slope_x: float32 [16384], P('road'), may hold values from -0.3 to 0.3
- road_slope_y: float32 [16384], P('road'), may hold values from -0.3 to 0.3
- road_stiff: float32 [16384], P('road'), may hold values from 1 to 4
- tile_list: int32 [8, 4, 4], P('blk', 'road'), may hold values from 0 to 63, as said below
- pair_node: int32 [8, 4, 8192], P('blk', 'road'), may hold values from 0 to 2047, as said below
- pair_slot: int32 [8, 4, 8192], P('blk', 'road'), may hold values from 0 to 1023, as said below
- pair_count: int32 [8, 4], P('blk', 'road'), may hold values from 0 to 8192, as said below
Outputs:
- veloc_out: float32 [3, 16, 64, 1024], P(None, None, 'road', 'blk')
- road_load: float32 [16384], P(('blk', 'road'))
Inputs may be any that keep to these rules, and one draw needn't show every extreme that they name: `pair_count`: the sectors with live slots form one run of 1 consecutive sectors round the cycle, possibly across its end; on their devices from 4096 to 8192 slots are live, and some device has all 8192 live; on all other devices none. Index of a node of the device's own outer layer: lateral position pair_node // 128, circumferential position pair_node % 128 within the device's block. Position within the device's listed tiles: tile pair_slot // 256, facet pair_slot % 256 of that tile. `tile_list`: 4 consecutive tile numbers counted modulo 64; tile t holds facets t * 256 to t * 256 + 255, on road patch t // 16.
All inputs are finite; a program needn't handle non-finite values.
Results may differ from a plain program's by a relative error of at most 0.0001.
Values sent between devices are 32-bit elements; how exact they have to be, the bound alone decides.
A program may use at most 64 MiB of HBM per device.

v0:
```python
import functools

import jax
import jax.numpy as jnp
from jax import lax
from jax.experimental import pallas as pl
from jax.experimental.pallas import tpu as pltpu
from jax.sharding import PartitionSpec as P

TILE = 256
LANES = 128
GROUP = 1024

hardening = 0.5
time_step = 0.25

MESH = pl.DeviceIdType.MESH
NT = (((1,), (1,)), ((), ()))


def split_two(x):
    high = x.astype(jnp.bfloat16).astype(jnp.float32)
    return high, x - high


def tension(weights, strain):
    squared = strain[0] * strain[0] + strain[1] * strain[1] + strain[2] * strain[2]
    scaled = weights * (1.0 + hardening * squared)
    return [scaled * s for s in strain]


def kernel(
    n_blk,
    n_road,
    lat,
    in_kernel_sum,
    disp_in,
    veloc_in,
    stiff_in,
    mass_in,
    height,
    slope_x,
    slope_y,
    road_stiff,
    tiles,
    nodes_in,
    slots_in,
    count,
    v_out,
    load_out,
    disp,
    veloc,
    stiff,
    mass,
    nodes,
    slots,
    in_sems,
    own_sems,
    picked_vals,
    normals,
    u1,
    v1,
    force,
    node_hot,
    facet_hot,
    facet_vals,
    facet_all,
    table,
    up_send,
    down_send,
    up_recv,
    down_recv,
    side_up_send,
    side_down_send,
    side_up_recv,
    side_down_recv,
    halo_sems,
    facet_sems,
    *reduction,
):
    b = lax.axis_index("blk")
    r = lax.axis_index("road")
    rows = disp.shape[1]
    layers = rows // lat
    groups = nodes.shape[1] // GROUP
    n_rows = table.shape[1]
    half = table.shape[1] // tiles.shape[1]
    patch_rows = height.shape[0]

    def road_peer(offset):
        return {"blk": b, "road": lax.rem(r + offset, n_road)}

    def blk_peer(offset):
        return {"blk": lax.rem(b + offset, n_blk), "road": r}

    blk_offsets = range(1, n_blk) if in_kernel_sum else sorted({1, n_blk - 1})
    barrier = pltpu.get_barrier_semaphore()
    for offset in blk_offsets:
        pl.semaphore_signal(barrier, inc=1, device_id=blk_peer(offset), device_id_type=MESH)
    for offset in range(1, n_road):
        pl.semaphore_signal(barrier, inc=1, device_id=road_peer(offset), device_id_type=MESH)

    def fill_faces(step, source):
        for c in range(3):
            turned = source[c].T
            up_send[step, c : c + 1, :] = turned[LANES - 1 : LANES, :]
            down_send[step, c : c + 1, :] = turned[0:1, :]
            side_up_send[step, c] = source[c, pl.ds(lat - 1, layers, stride=lat), :]
            side_down_send[step, c] = source[c, pl.ds(0, layers, stride=lat), :]
        if step == 0:
            down_send[step, 3:4, :] = stiff[2].T[0:1, :]
            side_down_send[step, 3] = stiff[1, pl.ds(0, layers, stride=lat), :]

    def halo_copies(step):
        plan = (
            (up_send, up_recv, blk_peer(1)),
            (down_send, down_recv, blk_peer(n_blk - 1)),
            (side_up_send, side_up_recv, road_peer(1)),
            (side_down_send, side_down_recv, road_peer(n_road - 1)),
        )
        return [
            pltpu.make_async_remote_copy(
                src_ref=src.at[step],
                dst_ref=dst.at[step],
                send_sem=halo_sems.at[step, 0, i],
                recv_sem=halo_sems.at[step, 1, i],
                device_id=peer,
                device_id_type=MESH,
            )
            for i, (src, dst, peer) in enumerate(plan)
        ]

    loads_in = [
        pltpu.make_async_copy(src, dst, in_sems.at[i])
        for i, (src, dst) in enumerate(
            (
                (disp_in, disp),
                (stiff_in, stiff),
                (nodes_in, nodes),
                (slots_in, slots),
                (mass_in, mass),
                (veloc_in, veloc),
            )
        )
    ]
    for copy in loads_in:
        copy.start()
    own = (height, slope_x, slope_y, road_stiff)
    own_copies = [
        pltpu.make_async_copy(own[a], facet_all.at[a * n_road + r], own_sems.at[a]) for a in range(4)
    ]
    for copy in own_copies:
        copy.start()
    for copy in loads_in[:2]:
        copy.wait()
    fill_faces(0, disp)
    for copy in loads_in[2:4]:
        copy.wait()

    def make_hot(g, _):
        at = pl.ds(pl.multiple_of(g * GROUP, GROUP), GROUP)
        lane = lax.broadcasted_iota(jnp.int32, (LANES, GROUP), 0)
        node_lane = nodes[:, at] & (LANES - 1)
        slot_lane = slots[:, at] & (LANES - 1)
        node_hot[g] = jnp.where(lane == node_lane, 1.0, 0.0).astype(jnp.bfloat16)
        facet_hot[g] = jnp.where(lane == slot_lane, 1.0, 0.0).astype(jnp.bfloat16)
        return 0

    lax.fori_loop(0, groups, make_hot, 0, unroll=2)

    pl.semaphore_wait(barrier, len(blk_offsets) + n_road - 1)
    halos0 = halo_copies(0)
    for copy in halos0:
        copy.start()
    facet_copies = []
    for offset in range(1, n_road):
        for a in range(4):
            copy = pltpu.make_async_remote_copy(
                src_ref=own[a],
                dst_ref=facet_all.at[a * n_road + r],
                send_sem=facet_sems.at[0, a, offset - 1],
                recv_sem=facet_sems.at[1, a, offset - 1],
                device_id=road_peer(offset),
                device_id_type=MESH,
            )
            copy.start()
            facet_copies.append(copy)
    lat_index = lax.broadcasted_iota(jnp.int32, (lat, LANES), 0)
    lane_index = lax.broadcasted_iota(jnp.int32, (lat, LANES), 1)

    def layer_rows(k):
        return pl.ds(pl.multiple_of(k * lat, lat), lat)

    def inside(source, k, above, rim):
        at = layer_rows(k)
        u = [source[c, at, :] for c in range(3)]
        if rim:
            strain = u
        else:
            below = layer_rows(k - 1)
            strain = [u[c] - source[c, below, :] for c in range(3)]
        radial = tension(stiff[0, at, :], strain)
        side = tension(stiff[1, at, :], [x - pltpu.roll(x, 1, 0) for x in u])
        around = tension(stiff[2, at, :], [x - pltpu.roll(x, 1, 1) for x in u])
        for c in range(3):
            t = jnp.where(lat_index == 0, 0.0, side[c])
            w = jnp.where(lane_index == 0, 0.0, around[c])
            force[c, at, :] = (
                (above[c] - radial[c])
                + (pltpu.roll(t, lat - 1, 0) - t)
                + (pltpu.roll(w, LANES - 1, 1) - w)
            )
        return radial

    def interior(source):
        nothing = tuple(jnp.zeros((lat, LANES), jnp.float32) for _ in range(3))

        def body(i, above):
            return tuple(inside(source, layers - 1 - i, above, False))

        above = lax.fori_loop(0, layers - 1, body, nothing, unroll=3)
        inside(source, 0, above, True)

    def rim_force(step):
        stiff_around = down_recv[0, 3:4, :]
        own_around = down_send[0, 3:4, :]
        low = tension(own_around, [down_send[step, c : c + 1, :] - up_recv[step, c : c + 1, :] for c in range(3)])
        high = tension(stiff_around, [down_recv[step, c : c + 1, :] - up_send[step, c : c + 1, :] for c in range(3)])
        place = lax.broadcasted_iota(jnp.int32, (LANES, rows), 0)
        for c in range(3):
            turned = jnp.where(place == 0, -low[c], jnp.where(place == LANES - 1, high[c], 0.0))
            force[c] = force[c] + turned.T
        first = jnp.where(r == 0, 0.0, 1.0)
        last = jnp.where(r == n_road - 1, 0.0, 1.0)
        low = tension(
            side_down_send[0, 3], [side_down_send[step, c] - first * side_up_recv[step, c] for c in range(3)]
        )
        high = tension(
            last * side_down_recv[0, 3], [side_down_recv[step, c] - side_up_send[step, c] for c in range(3)]
        )
        for c in range(3):
            at = pl.ds(0, layers, stride=lat)
            force[c, at, :] = force[c, at, :] - low[c]
            at = pl.ds(lat - 1, layers, stride=lat)
            force[c, at, :] = force[c, at, :] + high[c]

    live_count = count[0, 0]

    node_row = lax.broadcasted_iota(jnp.int32, (lat, GROUP), 0)
    facet_row = lax.broadcasted_iota(jnp.int32, (n_rows, GROUP), 0)
    slot_lane = lax.broadcasted_iota(jnp.int32, (1, GROUP), 1)

    def split_rows(arrays):
        parts = [split_two(x) for x in arrays]
        return jnp.concatenate([p[0] for p in parts] + [p[1] for p in parts], axis=0).astype(jnp.bfloat16)

    def group_at(g):
        return pl.ds(pl.multiple_of(g * GROUP, GROUP), GROUP)

    def look(table_rows, hot, mask, height_of):
        found = jnp.dot(table_rows, hot, preferred_element_type=jnp.float32)
        arrays = found.shape[0] // (2 * height_of)
        out = []
        for a in range(arrays):
            both = (
                found[a * height_of : (a + 1) * height_of]
                + found[(arrays + a) * height_of : (arrays + a + 1) * height_of]
            )
            out.append(jnp.sum(jnp.where(mask, both, 0.0), axis=0, keepdims=True))
        return out

    def outer_rows(source):
        return split_rows([source[c, rows - lat : rows, :] for c in range(3)])

    def on_nodes(g):
        return node_row == (nodes[:, group_at(g)] >> 7)

    def press(g, u, h, sx, sy, ks):
        live = slot_lane + g * GROUP < live_count
        return jnp.where(live, ks * jnp.maximum(h + sx * u[0] + sy * u[1] - u[2], 0.0), 0.0)

    def gather_force(g, on_node, sx, sy, normal, pushed):
        high, low = zip(*[split_two(x) for x in (-sx * normal, -sy * normal, normal)])
        spread = jnp.concatenate([jnp.where(on_node, x, 0.0) for x in high + low], axis=0)
        return pushed + lax.dot_general(
            spread.astype(jnp.bfloat16), node_hot[g], NT, preferred_element_type=jnp.float32
        )

    def gather_load(g, on_facet, normal, loads):
        heaped = jnp.concatenate([jnp.where(on_facet, x, 0.0) for x in split_two(normal)], axis=0)
        return loads + lax.dot_general(
            heaped.astype(jnp.bfloat16), facet_hot[g], NT, preferred_element_type=jnp.float32
        )

    def on_facets(g):
        return facet_row == (slots[:, group_at(g)] >> 7)

    def stored_facet(g, a):
        return facet_vals[g, a : a + 1, :]

    no_push = jnp.zeros((6 * lat, LANES), jnp.float32)

    def outer_sum(pushed):
        return [pushed[c * lat : (c + 1) * lat] + pushed[(3 + c) * lat : (4 + c) * lat] for c in range(3)]

    def add_outer(outer_force):
        for c in range(3):
            force[c, rows - lat : rows, :] = force[c, rows - lat : rows, :] + outer_force[c]

    interior(disp)
    first_outer = outer_rows(disp)

    def pick_first(g, _):
        for c, x in enumerate(look(first_outer, node_hot[g], on_nodes(g), lat)):
            picked_vals[g, c : c + 1, :] = x
        return 0

    lax.fori_loop(0, groups, pick_first, 0, unroll=4)

    for copy in own_copies + loads_in[4:]:
        copy.wait()
    for copy in halos0:
        copy.wait()
    rim_force(0)

    def advance(k, _):
        at = layer_rows(k)
        scale = time_step / mass[at, :]
        for c in range(3):
            v = veloc[c, at, :] + scale * force[c, at, :]
            v1[c, at, :] = v
            u1[c, at, :] = disp[c, at, :] + time_step * v
        return 0

    lax.fori_loop(0, layers - 1, advance, 0)

    for copy in facet_copies:
        copy.wait()
    for j in range(tiles.shape[1]):
        for i in range(half):
            row = tiles[0, j] * half + i
            for a in range(4):
                table[a, j * half + i : j * half + i + 1, :] = facet_all[
                    a * n_road + row // patch_rows, pl.ds(row % patch_rows, 1), :
                ]
    looked_from = split_rows([table[a] for a in range(4)])

    def first_contact(g, pushed):
        values = look(looked_from, facet_hot[g], on_facets(g), n_rows)
        for a in range(4):
            facet_vals[g, a : a + 1, :] = values[a]
        h, sx, sy, ks = values
        normal = press(g, [picked_vals[g, c : c + 1, :] for c in range(3)], h, sx, sy, ks)
        normals[g, 0:1, :] = normal
        return gather_force(g, on_nodes(g), sx, sy, normal, pushed)

    add_outer(outer_sum(lax.fori_loop(0, groups, first_contact, no_push, unroll=4)))
    advance(layers - 1, 0)

    second_outer = outer_rows(u1)

    def second_press(g, loads):
        u = look(second_outer, node_hot[g], on_nodes(g), lat)
        normal = press(g, u, *[stored_facet(g, a) for a in range(4)])
        normals[g, 1:2, :] = normal
        return gather_load(g, on_facets(g), normal + normals[g, 0:1, :], loads)

    loads = lax.fori_loop(
        0, groups, second_press, jnp.zeros((2 * n_rows, LANES), jnp.float32), unroll=4
    )
    loads = loads[:n_rows] + loads[n_rows:]

    def dense(shape, row_of):
        row = row_of(shape)
        total = jnp.zeros(shape, jnp.float32)
        for j in range(n_rows):
            here = tiles[0, j // half] * half + j % half
            line = loads[j : j + 1, :].reshape((1,) * (len(shape) - 1) + (LANES,))
            total = total + jnp.where(row == here, line, 0.0)
        return total

    if in_kernel_sum:
        spread_out, road_recv, reduced, blk_recv, road_sems, blk_sems = reduction
        chunk_rows = load_out.shape[0]
        for to in range(n_road):
            spread_out[to] = dense(
                (n_blk, chunk_rows, LANES),
                lambda s: (lax.broadcasted_iota(jnp.int32, s, 0) * n_road + to) * chunk_rows
                + lax.broadcasted_iota(jnp.int32, s, 1),
            )
        road_copies = []
        for offset in range(1, n_road):
            copy = pltpu.make_async_remote_copy(
                src_ref=spread_out.at[lax.rem(r + offset, n_road)],
                dst_ref=road_recv.at[offset - 1],
                send_sem=road_sems.at[0, offset - 1],
                recv_sem=road_sems.at[1, offset - 1],
                device_id=road_peer(offset),
                device_id_type=MESH,
            )
            copy.start()
            road_copies.append(copy)
    else:
        load_out[...] = dense(load_out.shape, lambda s: lax.broadcasted_iota(jnp.int32, s, 0))

    fill_faces(1, u1)
    halos1 = halo_copies(1)
    for copy in halos1:
        copy.start()
    interior(u1)

    if in_kernel_sum:
        for copy in road_copies:
            copy.wait()
        total = spread_out[r]
        for i in range(n_road - 1):
            total = total + road_recv[i]
        reduced[...] = total
        blk_copies = []
        for offset in range(1, n_blk):
            copy = pltpu.make_async_remote_copy(
                src_ref=reduced.at[lax.rem(b + offset, n_blk)],
                dst_ref=blk_recv.at[offset - 1],
                send_sem=blk_sems.at[0, offset - 1],
                recv_sem=blk_sems.at[1, offset - 1],
                device_id=blk_peer(offset),
                device_id_type=MESH,
            )
            copy.start()
            blk_copies.append(copy)

    def second_contact(g, pushed):
        return gather_force(
            g, on_nodes(g), stored_facet(g, 1), stored_facet(g, 2), normals[g, 1:2, :], pushed
        )

    add_outer(outer_sum(lax.fori_loop(0, groups, second_contact, no_push, unroll=4)))
    for copy in halos1:
        copy.wait()
    rim_force(1)

    def finish(k, _):
        at = layer_rows(k)
        scale = time_step / mass[at, :]
        for c in range(3):
            v_out[c, at, :] = v1[c, at, :] + scale * force[c, at, :]
        return 0

    lax.fori_loop(0, layers, finish, 0)

    if in_kernel_sum:
        for copy in blk_copies:
            copy.wait()
        total = reduced[b]
        for i in range(n_blk - 1):
            total = total + blk_recv[i]
        load_out[...] = total


def on_device(
    n_blk,
    n_road,
    disp,
    veloc,
    stiff,
    mass,
    road_height,
    road_slope_x,
    road_slope_y,
    road_stiff,
    tile_list,
    pair_node,
    pair_slot,
    pair_count,
):
    _, layers, lat, lanes = disp.shape
    rows = layers * lat
    pairs = pair_node.shape[-1]
    groups = pairs // GROUP
    tiles_need = tile_list.shape[-1]
    patch_rows = road_height.shape[0] // LANES
    total_rows = patch_rows * n_road
    table_rows = tiles_need * TILE // LANES
    devices = n_blk * n_road
    in_kernel_sum = total_rows % devices == 0
    f32 = jnp.float32
    if in_kernel_sum:
        load_shape = (total_rows // devices, LANES)
    else:
        load_shape = (total_rows, LANES)
    scratch = [
        pltpu.VMEM((3, rows, lanes), f32),
        pltpu.VMEM((3, rows, lanes), f32),
        pltpu.VMEM((3, rows, lanes), f32),
        pltpu.VMEM((rows, lanes), f32),
        pltpu.VMEM((1, pairs), jnp.int32),
        pltpu.VMEM((1, pairs), jnp.int32),
        pltpu.SemaphoreType.DMA((6,)),
        pltpu.SemaphoreType.DMA((4,)),
        pltpu.VMEM((groups, 3, GROUP), f32),
        pltpu.VMEM((groups, 2, GROUP), f32),
        pltpu.VMEM((3, rows, lanes), f32),
        pltpu.VMEM((3, rows, lanes), f32),
        pltpu.VMEM((3, rows, lanes), f32),
        pltpu.VMEM((groups, LANES, GROUP), jnp.bfloat16),
        pltpu.VMEM((groups, LANES, GROUP), jnp.bfloat16),
        pltpu.VMEM((groups, 4, GROUP), f32),
        pltpu.VMEM((4 * n_road, patch_rows, LANES), f32),
        pltpu.VMEM((4, table_rows, LANES), f32),
        pltpu.VMEM((2, 3, rows), f32),
        pltpu.VMEM((2, 4, rows), f32),
        pltpu.VMEM((2, 3, rows), f32),
        pltpu.VMEM((2, 4, rows), f32),
        pltpu.VMEM((2, 3, layers, lanes), f32),
        pltpu.VMEM((2, 4, layers, lanes), f32),
        pltpu.VMEM((2, 3, layers, lanes), f32),
        pltpu.VMEM((2, 4, layers, lanes), f32),
        pltpu.SemaphoreType.DMA((2, 2, 4)),
        pltpu.SemaphoreType.DMA((2, 4, n_road - 1)),
    ]
    if in_kernel_sum:
        scratch += [
            pltpu.VMEM((n_road, n_blk) + load_shape, f32),
            pltpu.VMEM((n_road - 1, n_blk) + load_shape, f32),
            pltpu.VMEM((n_blk,) + load_shape, f32),
            pltpu.VMEM((n_blk - 1,) + load_shape, f32),
            pltpu.SemaphoreType.DMA((2, n_road - 1)),
            pltpu.SemaphoreType.DMA((2, n_blk - 1)),
        ]
    vmem = pl.BlockSpec(memory_space=pltpu.VMEM)
    hbm = pl.BlockSpec(memory_space=pl.ANY)
    smem = pl.BlockSpec(memory_space=pltpu.SMEM)
    velocity, load = pl.pallas_call(
        functools.partial(kernel, n_blk, n_road, lat, in_kernel_sum),
        out_shape=(
            pltpu.VMEM((3, rows, lanes), f32),
            pltpu.VMEM(load_shape, f32),
        ),
        in_specs=[hbm] * 8 + [smem, hbm, hbm, smem],
        out_specs=(vmem, vmem),
        scratch_shapes=scratch,
        compiler_params=pltpu.CompilerParams(collective_id=0, has_side_effects=True),
    )(
        disp.reshape(3, rows, lanes),
        veloc.reshape(3, rows, lanes),
        stiff.reshape(3, rows, lanes),
        mass.reshape(rows, lanes),
        road_height.reshape(patch_rows, LANES),
        road_slope_x.reshape(patch_rows, LANES),
        road_slope_y.reshape(patch_rows, LANES),
        road_stiff.reshape(patch_rows, LANES),
        tile_list.reshape(1, tiles_need),
        pair_node.reshape(1, pairs),
        pair_slot.reshape(1, pairs),
        pair_count.reshape(1, 1),
    )
    load = load.reshape(-1)
    if not in_kernel_sum:
        load = lax.psum_scatter(load, ("blk", "road"), scatter_dimension=0, tiled=True)
    return velocity.reshape(disp.shape), load


def solution(mesh):
    in_specs = (
        P(None, None, "road", "blk"),
        P(None, None, "road", "blk"),
        P(None, None, "road", "blk"),
        P(None, "road", "blk"),
        P("road"),
        P("road"),
        P("road"),
        P("road"),
        P("blk", "road", None),
        P("blk", "road", None),
        P("blk", "road", None),
        P("blk", "road"),
    )
    out_specs = (P(None, None, "road", "blk"), P(("blk", "road")))
    body = functools.partial(on_device, mesh.shape["blk"], mesh.shape["road"])
    return jax.shard_map(body, mesh=mesh, in_specs=in_specs, out_specs=out_specs, check_vma=False)
```

profile of v0, /device:TPU:0, one launch (start us, length us, event | category | flops | bytes accessed | tf_op | source)
XLA Modules:
  0.0 25.9 jit_solution(11738864257894957561)
XLA Ops:
  1.3 23.3 %shard_map.131 = (f32[3,256,128]{2,1,0:T(8,128)S(1)}, f32[4,128]{1,0:T(4,128)S(1)}) custom-call(f32[3,256,128]{2,1,0:T(8,128)} %bitcast.15, f32[3,256,128]{2,1,0:T(8,128)} %bitcast.16, f32[3,256,128]{2,1,0:T(8,128)} %bitcast.17, f32[256,128]{1,0:T(8,128)} %bitcast.18, f32[32,128]{1,0:T(8,128)} %bitcast.21, f32[32,128]{1,0:T(8,128)} %bitcast.22, ...), custom_call_target="tpu_custom_call" | custom-call | tf_op jit(solution)/shard_map/pallas_call | solution.py:533
  24.6 0.7 %copy.16 = f32[3,16,16,128]{3,2,1,0:T(8,128)} copy(f32[3,16,16,128]{3,2,1,0:T(8,128)S(1)} %bitcast.13) | data formatting | bytes 786432
  25.3 0.6 %copy.17 = f32[512]{0:T(512)} copy(f32[512]{0:T(512)S(1)} %bitcast.14) | data formatting | bytes 4096
where the time goes:
time: 26.1 us; the launch traced here: 25.9 us
  Pallas kernels  23.3 us (89%)
  local copies, waits for them, and re-layouts  1.33 us (5%)
  between operations  1.29 us (5%)
    pallas_call x1, Pallas kernels, on_device(): pl.pallas_call(functools.partial(kernel, n_blk, n_road, lat, in_kernel_su...  23.3 us
    unnamed x2, local copies, waits for them, and re-layouts  1.33 us

commit v1 on v0

v1 whole, which is shorter than its diff:
```python
import functools

import jax
import jax.numpy as jnp
from jax import lax
from jax.experimental import pallas as pl
from jax.experimental.pallas import tpu as pltpu
from jax.sharding import PartitionSpec as P

TILE = 256
LANES = 128
SUB = 8

hardening = 0.5
time_step = 0.25

MESH = pl.DeviceIdType.MESH
NT = (((1,), (1,)), ((), ()))


def split_two(x):
    high = x.astype(jnp.bfloat16).astype(jnp.float32)
    return high, x - high


def tension(weights, strain):
    squared = strain[0] * strain[0] + strain[1] * strain[1] + strain[2] * strain[2]
    scaled = weights * (1.0 + hardening * squared)
    return [scaled * s for s in strain]


def kernel(
    n_blk,
    n_road,
    lat,
    in_kernel_sum,
    disp_in,
    veloc_in,
    stiff_in,
    mass_in,
    height,
    slope_x,
    slope_y,
    road_stiff,
    tiles_in,
    nodes_in,
    slots_in,
    count_in,
    v_out,
    load_out,
    disp,
    veloc,
    stiff,
    mass,
    nodes,
    slots,
    tiles,
    count,
    in_sems,
    own_sems,
    picked,
    facet_vals,
    normals,
    parts,
    u1,
    v1,
    force,
    scale,
    rim,
    side,
    facet_all,
    table,
    up_send,
    down_send,
    up_recv,
    down_recv,
    side_up_send,
    side_down_send,
    side_up_recv,
    side_down_recv,
    halo_sems,
    facet_sems,
    *reduction,
):
    b = lax.axis_index("blk")
    r = lax.axis_index("road")
    rows = disp.shape[1]
    layers = rows // lat
    groups = nodes.shape[0] // SUB
    n_rows = table.shape[1]
    tiles_need = tiles.shape[1]
    half = n_rows // tiles_need
    patch_rows = height.shape[0]

    def road_peer(offset):
        return {"blk": b, "road": lax.rem(r + offset, n_road)}

    def blk_peer(offset):
        return {"blk": lax.rem(b + offset, n_blk), "road": r}

    blk_offsets = range(1, n_blk) if in_kernel_sum else sorted({1, n_blk - 1})
    barrier = pltpu.get_barrier_semaphore()
    for offset in reversed(blk_offsets):
        pl.semaphore_signal(barrier, inc=1, device_id=blk_peer(offset), device_id_type=MESH)
    for offset in range(1, n_road):
        pl.semaphore_signal(barrier, inc=1, device_id=road_peer(offset), device_id_type=MESH)

    def fill_faces(step, source):
        for c in range(3):
            turned = source[c].T
            up_send[step, c : c + 1, :] = turned[LANES - 1 : LANES, :]
            down_send[step, c : c + 1, :] = turned[0:1, :]
            side_up_send[step, c] = source[c, pl.ds(lat - 1, layers, stride=lat), :]
            side_down_send[step, c] = source[c, pl.ds(0, layers, stride=lat), :]
        if step == 0:
            down_send[step, 3:4, :] = stiff[2].T[0:1, :]
            side_down_send[step, 3] = stiff[1, pl.ds(0, layers, stride=lat), :]

    def halo_copies(step):
        plan = (
            (up_send, up_recv, blk_peer(1)),
            (down_send, down_recv, blk_peer(n_blk - 1)),
            (side_up_send, side_up_recv, road_peer(1)),
            (side_down_send, side_down_recv, road_peer(n_road - 1)),
        )
        return [
            pltpu.make_async_remote_copy(
                src_ref=src.at[step],
                dst_ref=dst.at[step],
                send_sem=halo_sems.at[step, 0, i],
                recv_sem=halo_sems.at[step, 1, i],
                device_id=peer,
                device_id_type=MESH,
            )
            for i, (src, dst, peer) in enumerate(plan)
        ]

    loads_in = [
        pltpu.make_async_copy(src, dst, in_sems.at[i])
        for i, (src, dst) in enumerate(
            (
                (disp_in, disp),
                (stiff_in, stiff),
                (nodes_in, nodes),
                (mass_in, mass),
                (veloc_in, veloc),
                (slots_in, slots),
                (tiles_in, tiles),
                (count_in, count),
            )
        )
    ]
    for copy in loads_in:
        copy.start()
    own = (height, slope_x, slope_y, road_stiff)
    own_copies = [
        pltpu.make_async_copy(own[a], facet_all.at[a * n_road + r], own_sems.at[a]) for a in range(4)
    ]
    if in_kernel_sum:
        tiles_all, loads_all, reduced, blk_recv, tile_sems, road_sems, blk_sems = reduction
        own_copies.append(pltpu.make_async_copy(tiles_in, tiles_all.at[r], own_sems.at[4]))
    for copy in own_copies:
        copy.start()
    for copy in loads_in[:2]:
        copy.wait()
    fill_faces(0, disp)

    pl.semaphore_wait(barrier, len(blk_offsets) + n_road - 1)
    halos0 = halo_copies(0)
    for copy in halos0[:2]:
        copy.start()
    facet_copies = []
    for a in range(4):
        for offset in range(1, n_road):
            copy = pltpu.make_async_remote_copy(
                src_ref=own[a],
                dst_ref=facet_all.at[a * n_road + r],
                send_sem=facet_sems.at[0, a, offset - 1],
                recv_sem=facet_sems.at[1, a, offset - 1],
                device_id=road_peer(offset),
                device_id_type=MESH,
            )
            copy.start()
            facet_copies.append(copy)
    for copy in halos0[2:]:
        copy.start()
    tile_copies = []
    if in_kernel_sum:
        for offset in range(1, n_road):
            copy = pltpu.make_async_remote_copy(
                src_ref=tiles_in,
                dst_ref=tiles_all.at[r],
                send_sem=tile_sems.at[0, offset - 1],
                recv_sem=tile_sems.at[1, offset - 1],
                device_id=road_peer(offset),
                device_id_type=MESH,
            )
            copy.start()
            tile_copies.append(copy)

    lat_index = lax.broadcasted_iota(jnp.int32, (lat, LANES), 0)
    lane_index = lax.broadcasted_iota(jnp.int32, (lat, LANES), 1)

    def layer_rows(k):
        return pl.ds(pl.multiple_of(k * lat, lat), lat)

    def inside(source, k, above, bottom):
        at = layer_rows(k)
        u = [source[c, at, :] for c in range(3)]
        if bottom:
            strain = u
        else:
            below = layer_rows(k - 1)
            strain = [u[c] - source[c, below, :] for c in range(3)]
        radial = tension(stiff[0, at, :], strain)
        beside = tension(stiff[1, at, :], [x - pltpu.roll(x, 1, 0) for x in u])
        around = tension(stiff[2, at, :], [x - pltpu.roll(x, 1, 1) for x in u])
        for c in range(3):
            t = jnp.where(lat_index == 0, 0.0, beside[c])
            w = jnp.where(lane_index == 0, 0.0, around[c])
            force[c, at, :] = (
                (above[c] - radial[c])
                + (pltpu.roll(t, lat - 1, 0) - t)
                + (pltpu.roll(w, LANES - 1, 1) - w)
            )
        return radial

    def interior(source):
        nothing = tuple(jnp.zeros((lat, LANES), jnp.float32) for _ in range(3))

        def body(i, above):
            return tuple(inside(source, layers - 1 - i, above, False))

        above = lax.fori_loop(0, layers - 1, body, nothing, unroll=3)
        inside(source, 0, above, True)

    def fill_rim(step):
        stiff_around = down_recv[0, 3:4, :]
        own_around = down_send[0, 3:4, :]
        low = tension(own_around, [down_send[step, c : c + 1, :] - up_recv[step, c : c + 1, :] for c in range(3)])
        high = tension(stiff_around, [down_recv[step, c : c + 1, :] - up_send[step, c : c + 1, :] for c in range(3)])
        for c in range(3):
            for i in range(rows // LANES):
                piece = slice(i * LANES, (i + 1) * LANES)
                rim[c, i : i + 1, :] = -low[c][:, piece]
                rim[3 + c, i : i + 1, :] = high[c][:, piece]
        first = jnp.where(r == 0, 0.0, 1.0)
        last = jnp.where(r == n_road - 1, 0.0, 1.0)
        low = tension(
            side_down_send[0, 3], [side_down_send[step, c] - first * side_up_recv[step, c] for c in range(3)]
        )
        high = tension(
            last * side_down_recv[0, 3], [side_down_recv[step, c] - side_up_send[step, c] for c in range(3)]
        )
        for c in range(3):
            side[c] = -low[c]
            side[3 + c] = high[c]

    def lanes_of(row, index):
        return jnp.take_along_axis(
            jnp.broadcast_to(row, index.shape), index, axis=1, mode="promise_in_bounds"
        )

    def rim_force(k, c):
        start = k * lat
        place = lat_index + lax.rem(start, LANES)
        line = pl.ds(start // LANES, 1)
        turned = jnp.where(
            lane_index == 0,
            lanes_of(rim[c, line, :], place),
            jnp.where(lane_index == LANES - 1, lanes_of(rim[3 + c, line, :], place), 0.0),
        )
        edge = jnp.where(
            lat_index == 0,
            side[c, pl.ds(k, 1), :],
            jnp.where(lat_index == lat - 1, side[3 + c, pl.ds(k, 1), :], 0.0),
        )
        return turned + edge

    node_row = lax.broadcasted_iota(jnp.int16, (lat, LANES), 0)
    lane_16 = lax.broadcasted_iota(jnp.int16, (LANES, LANES), 0)
    facet_row = lax.broadcasted_iota(jnp.int16, (2 * n_rows, LANES), 0)
    facet_low = facet_row >= n_rows
    facet_row = jnp.where(facet_low, facet_row - jnp.int16(n_rows), facet_row)
    one = jnp.ones((LANES, LANES), jnp.bfloat16)
    none = jnp.zeros((LANES, LANES), jnp.bfloat16)
    slot_index = lax.broadcasted_iota(jnp.int32, (SUB, LANES), 0) * LANES + lax.broadcasted_iota(
        jnp.int32, (SUB, LANES), 1
    )

    def group_at(g):
        return pl.ds(pl.multiple_of(g * SUB, SUB), SUB)

    def look(lines, index):
        row, lane = index >> 7, index & (LANES - 1)
        found = None
        for i, line in enumerate(lines):
            here = [lanes_of(x, lane) for x in line]
            found = here if i == 0 else [jnp.where(row == i, x, y) for x, y in zip(here, found)]
        return found

    def pick(source, g):
        lines = [[source[c, rows - lat + i : rows - lat + i + 1, :] for c in range(3)] for i in range(lat)]
        return look(lines, nodes[group_at(g), :])

    def pick_facet(g):
        lines = [[table[a, i : i + 1, :] for a in range(4)] for i in range(n_rows)]
        return look(lines, slots[group_at(g), :])

    def press(g, u, h, sx, sy, ks):
        live = slot_index + g * (SUB * LANES) < count[0, 0]
        return jnp.where(live, ks * jnp.maximum(h + sx * u[0] + sy * u[1] - u[2], 0.0), 0.0)

    def wide(ref_row, height_of, dtype):
        return jnp.broadcast_to(ref_row, (height_of, LANES)).astype(dtype)

    def hot(ref, row):
        return jnp.where(lane_16 == wide(ref[pl.ds(row, 1), :] & (LANES - 1), LANES, jnp.int16), one, none)

    def scatter_force(step, g, pushed):
        at = group_at(g)
        normal = normals[step, at, :]
        values = (-facet_vals[1, at, :] * normal, -facet_vals[2, at, :] * normal, normal)
        high, low = zip(*[split_two(x) for x in values])
        for i, x in enumerate(high + low):
            parts[i, at, :] = x
        spread, hots = [], []
        for s in range(SUB):
            row = g * SUB + s
            mask = node_row == wide(nodes[pl.ds(row, 1), :] >> 7, lat, jnp.int16)
            spread.append(
                jnp.concatenate(
                    [
                        jnp.where(mask, wide(parts[i, pl.ds(row, 1), :], lat, jnp.bfloat16), none[:lat])
                        for i in range(6)
                    ],
                    axis=0,
                )
            )
            hots.append(hot(nodes, row))
        return pushed + lax.dot_general(
            jnp.concatenate(spread, axis=1), jnp.concatenate(hots, axis=1), NT, preferred_element_type=jnp.float32
        )

    def scatter_load(g, loads):
        at = group_at(g)
        high, low = split_two(normals[0, at, :] + normals[1, at, :])
        parts[6, at, :] = high
        parts[7, at, :] = low
        spread, hots = [], []
        for s in range(SUB):
            row = g * SUB + s
            mask = facet_row == wide(slots[pl.ds(row, 1), :] >> 7, 2 * n_rows, jnp.int16)
            both = jnp.where(
                facet_low,
                wide(parts[7, pl.ds(row, 1), :], 2 * n_rows, jnp.bfloat16),
                wide(parts[6, pl.ds(row, 1), :], 2 * n_rows, jnp.bfloat16),
            )
            spread.append(jnp.where(mask, both, jnp.zeros((2 * n_rows, LANES), jnp.bfloat16)))
            hots.append(hot(slots, row))
        return loads + lax.dot_general(
            jnp.concatenate(spread, axis=1), jnp.concatenate(hots, axis=1), NT, preferred_element_type=jnp.float32
        )

    no_push = jnp.zeros((6 * lat, LANES), jnp.float32)

    def add_outer(pushed):
        for c in range(3):
            here = pushed[c * lat : (c + 1) * lat] + pushed[(3 + c) * lat : (4 + c) * lat]
            force[c, rows - lat : rows, :] = force[c, rows - lat : rows, :] + here

    for copy in loads_in[2:5]:
        copy.wait()
    interior(disp)

    def pick_first(g, _):
        for c, x in enumerate(pick(disp, g)):
            picked[c, group_at(g), :] = x
        return 0

    lax.fori_loop(0, groups, pick_first, 0, unroll=2)

    def fill_scale(k, _):
        at = layer_rows(k)
        scale[at, :] = time_step / mass[at, :]
        return 0

    lax.fori_loop(0, layers, fill_scale, 0, unroll=2)

    for copy in loads_in[5:] + own_copies + facet_copies:
        copy.wait()
    for j in range(tiles_need):
        for i in range(half):
            row = tiles[0, j] * half + i
            for a in range(4):
                table[a, j * half + i : j * half + i + 1, :] = facet_all[
                    a * n_road + row // patch_rows, pl.ds(row % patch_rows, 1), :
                ]

    def first_press(g, _):
        at = group_at(g)
        values = pick_facet(g)
        for a in range(4):
            facet_vals[a, at, :] = values[a]
        normals[0, at, :] = press(g, [picked[c, at, :] for c in range(3)], *values)
        return 0

    lax.fori_loop(0, groups, first_press, 0, unroll=2)
    add_outer(lax.fori_loop(0, groups, functools.partial(scatter_force, 0), no_push, unroll=2))

    def advance(k, _):
        at = layer_rows(k)
        for c in range(3):
            v = veloc[c, at, :] + scale[at, :] * (force[c, at, :] + rim_force(k, c))
            v1[c, at, :] = v
            u1[c, at, :] = disp[c, at, :] + time_step * v
        return 0

    for copy in halos0:
        copy.wait()
    fill_rim(0)
    advance(layers - 1, 0)

    def second_press(g, _):
        at = group_at(g)
        normals[1, at, :] = press(g, pick(u1, g), *[facet_vals[a, at, :] for a in range(4)])
        return 0

    lax.fori_loop(0, groups, second_press, 0, unroll=2)
    loads = lax.fori_loop(0, groups, scatter_load, jnp.zeros((2 * n_rows, LANES), jnp.float32), unroll=2)
    loads = loads[:n_rows] + loads[n_rows:]

    if in_kernel_sum:
        loads_all[r] = loads
        road_copies = []
        for offset in range(1, n_road):
            copy = pltpu.make_async_remote_copy(
                src_ref=loads_all.at[r],
                dst_ref=loads_all.at[r],
                send_sem=road_sems.at[0, offset - 1],
                recv_sem=road_sems.at[1, offset - 1],
                device_id=road_peer(offset),
                device_id_type=MESH,
            )
            copy.start()
            road_copies.append(copy)
    else:
        row = lax.broadcasted_iota(jnp.int32, load_out.shape, 0)
        total = jnp.zeros(load_out.shape, jnp.float32)
        for j in range(n_rows):
            total = total + jnp.where(row == tiles[0, j // half] * half + j % half, loads[j : j + 1, :], 0.0)
        load_out[...] = total

    lax.fori_loop(0, layers - 1, advance, 0, unroll=3)
    fill_faces(1, u1)
    halos1 = halo_copies(1)
    for copy in halos1:
        copy.start()

    if in_kernel_sum:
        for copy in tile_copies + road_copies:
            copy.wait()
        chunk_rows = load_out.shape[0]
        row = lax.broadcasted_iota(jnp.int32, (n_blk * chunk_rows, LANES), 0)
        row = (row // chunk_rows * n_road + r) * chunk_rows + row % chunk_rows
        total = jnp.zeros((n_blk * chunk_rows, LANES), jnp.float32)
        for i in range(n_road):
            first_rows = tiles_all[i] * half
            for j in range(n_rows):
                here = first_rows[:, j // half : j // half + 1] + j % half
                total = total + jnp.where(row == here, loads_all[i, j : j + 1, :], 0.0)
        for i in range(n_blk):
            reduced[i] = total[i * chunk_rows : (i + 1) * chunk_rows]
        blk_copies = []
        for offset in range(1, n_blk):
            copy = pltpu.make_async_remote_copy(
                src_ref=reduced.at[lax.rem(b + offset, n_blk)],
                dst_ref=blk_recv.at[offset - 1],
                send_sem=blk_sems.at[0, offset - 1],
                recv_sem=blk_sems.at[1, offset - 1],
                device_id=blk_peer(offset),
                device_id_type=MESH,
            )
            copy.start()
            blk_copies.append(copy)

    interior(u1)
    add_outer(lax.fori_loop(0, groups, functools.partial(scatter_force, 1), no_push, unroll=2))
    for copy in halos1:
        copy.wait()
    fill_rim(1)

    def finish(k, _):
        at = layer_rows(k)
        for c in range(3):
            v_out[c, at, :] = v1[c, at, :] + scale[at, :] * (force[c, at, :] + rim_force(k, c))
        return 0

    lax.fori_loop(0, layers, finish, 0, unroll=2)

    if in_kernel_sum:
        for copy in blk_copies:
            copy.wait()
        total = reduced[b]
        for i in range(n_blk - 1):
            total = total + blk_recv[i]
        load_out[...] = total


def write_out(v_in, load_in, v_out, load_out, sems):
    copies = [
        pltpu.make_async_copy(src, dst, sems.at[i])
        for i, (src, dst) in enumerate(((v_in, v_out), (load_in, load_out)))
    ]
    for copy in copies:
        copy.start()
    for copy in copies:
        copy.wait()


def on_device(
    n_blk,
    n_road,
    disp,
    veloc,
    stiff,
    mass,
    road_height,
    road_slope_x,
    road_slope_y,
    road_stiff,
    tile_list,
    pair_node,
    pair_slot,
    pair_count,
):
    _, layers, lat, lanes = disp.shape
    rows = layers * lat
    pairs = pair_node.shape[-1]
    pair_rows = pairs // LANES
    tiles_need = tile_list.shape[-1]
    patch_rows = road_height.shape[0] // LANES
    total_rows = patch_rows * n_road
    table_rows = tiles_need * TILE // LANES
    devices = n_blk * n_road
    in_kernel_sum = total_rows % devices == 0
    f32 = jnp.float32
    if in_kernel_sum:
        load_shape = (total_rows // devices, LANES)
    else:
        load_shape = (total_rows, LANES)
    scratch = [
        pltpu.VMEM((3, rows, lanes), f32),
        pltpu.VMEM((3, rows, lanes), f32),
        pltpu.VMEM((3, rows, lanes), f32),
        pltpu.VMEM((rows, lanes), f32),
        pltpu.VMEM((pair_rows, LANES), jnp.int32),
        pltpu.VMEM((pair_rows, LANES), jnp.int32),
        pltpu.SMEM((1, tiles_need), jnp.int32),
        pltpu.SMEM((1, 1), jnp.int32),
        pltpu.SemaphoreType.DMA((8,)),
        pltpu.SemaphoreType.DMA((5,)),
        pltpu.VMEM((3, pair_rows, LANES), f32),
        pltpu.VMEM((4, pair_rows, LANES), f32),
        pltpu.VMEM((2, pair_rows, LANES), f32),
        pltpu.VMEM((8, pair_rows, LANES), f32),
        pltpu.VMEM((3, rows, lanes), f32),
        pltpu.VMEM((3, rows, lanes), f32),
        pltpu.VMEM((3, rows, lanes), f32),
        pltpu.VMEM((rows, lanes), f32),
        pltpu.VMEM((6, rows // LANES, LANES), f32),
        pltpu.VMEM((6, layers, lanes), f32),
        pltpu.VMEM((4 * n_road, patch_rows, LANES), f32),
        pltpu.VMEM((4, table_rows, LANES), f32),
        pltpu.VMEM((2, 3, rows), f32),
        pltpu.VMEM((2, 4, rows), f32),
        pltpu.VMEM((2, 3, rows), f32),
        pltpu.VMEM((2, 4, rows), f32),
        pltpu.VMEM((2, 3, layers, lanes), f32),
        pltpu.VMEM((2, 4, layers, lanes), f32),
        pltpu.VMEM((2, 3, layers, lanes), f32),
        pltpu.VMEM((2, 4, layers, lanes), f32),
        pltpu.SemaphoreType.DMA((2, 2, 4)),
        pltpu.SemaphoreType.DMA((2, 4, n_road - 1)),
    ]
    if in_kernel_sum:
        scratch += [
            pltpu.VMEM((n_road, 1, tiles_need), jnp.int32),
            pltpu.VMEM((n_road, table_rows, LANES), f32),
            pltpu.VMEM((n_blk,) + load_shape, f32),
            pltpu.VMEM((n_blk - 1,) + load_shape, f32),
            pltpu.SemaphoreType.DMA((2, n_road - 1)),
            pltpu.SemaphoreType.DMA((2, n_road - 1)),
            pltpu.SemaphoreType.DMA((2, n_blk - 1)),
        ]
    vmem = pl.BlockSpec(memory_space=pltpu.VMEM)
    hbm = pl.BlockSpec(memory_space=pltpu.HBM)
    anywhere = pl.BlockSpec(memory_space=pl.ANY)
    velocity, load = pl.pallas_call(
        functools.partial(kernel, n_blk, n_road, lat, in_kernel_sum),
        out_shape=(
            pltpu.VMEM((3, rows, lanes), f32),
            pltpu.VMEM(load_shape, f32),
        ),
        in_specs=[hbm] * 12,
        out_specs=(vmem, vmem),
        scratch_shapes=scratch,
        compiler_params=pltpu.CompilerParams(collective_id=0, has_side_effects=True),
    )(
        disp.reshape(3, rows, lanes),
        veloc.reshape(3, rows, lanes),
        stiff.reshape(3, rows, lanes),
        mass.reshape(rows, lanes),
        road_height.reshape(patch_rows, LANES),
        road_slope_x.reshape(patch_rows, LANES),
        road_slope_y.reshape(patch_rows, LANES),
        road_stiff.reshape(patch_rows, LANES),
        tile_list.reshape(1, tiles_need),
        pair_node.reshape(pair_rows, LANES),
        pair_slot.reshape(pair_rows, LANES),
        pair_count.reshape(1, 1),
    )
    velocity, load = pl.pallas_call(
        write_out,
        out_shape=(
            jax.ShapeDtypeStruct(velocity.shape, f32),
            jax.ShapeDtypeStruct(load.shape, f32),
        ),
        in_specs=[vmem] * 2,
        out_specs=(hbm, hbm),
        scratch_shapes=[pltpu.SemaphoreType.DMA((2,))],
    )(*(pltpu.with_memory_space_constraint(x, pltpu.VMEM) for x in (velocity, load)))
    load = load.reshape(-1)
    if not in_kernel_sum:
        load = lax.psum_scatter(load, ("blk", "road"), scatter_dimension=0, tiled=True)
    return velocity.reshape(disp.shape), load


def solution(mesh):
    in_specs = (
        P(None, None, "road", "blk"),
        P(None, None, "road", "blk"),
        P(None, None, "road", "blk"),
        P(None, "road", "blk"),
        P("road"),
        P("road"),
        P("road"),
        P("road"),
        P("blk", "road", None),
        P("blk", "road", None),
        P("blk", "road", None),
        P("blk", "road"),
    )
    out_specs = (P(None, None, "road", "blk"), P(("blk", "road")))
    body = functools.partial(on_device, mesh.shape["blk"], mesh.shape["road"])
    return jax.shard_map(body, mesh=mesh, in_specs=in_specs, out_specs=out_specs, check_vma=False)
```

time: 26.1 us -> 23.7 us (0.908)
  local copies, waits for them, and re-layouts: 1.33 us -> 0 us
  Pallas kernels: 23.3 us -> 22.3 us
    pallas_call x1, Pallas kernels: 23.3 us -> 21.5 us  [on_device(): pl.pallas_call(functools.partial(kernel, n_blk, n_road, lat, in_kernel_su...]
    unnamed x2 -> x0, local copies, waits for them, and re-layouts: 1.33 us -> none
    pallas_call x0 -> x1, Pallas kernels: none -> 0.77 us  [on_device(): pl.pallas_call(write_out, out_shape=(jax.ShapeDtypeStruct(velocity.shape,...]
where the time goes in v1:
time: 23.7 us; the launch traced here: 23.6 us
  Pallas kernels  22.3 us (94%)
  between operations  1.29 us (5%)
    pallas_call x1, Pallas kernels, on_device(): pl.pallas_call(functools.partial(kernel, n_blk, n_road, lat, in_kernel_su...  21.5 us
    pallas_call x1, Pallas kernels, on_device(): pl.pallas_call(write_out, out_shape=(jax.ShapeDtypeStruct(velocity.shape,...  0.77 us

profile of v1, /device:TPU:0, one launch (start us, length us, event | category | flops | bytes accessed | tf_op | source)
XLA Modules:
  0.0 23.6 jit_solution(7703298301467024687)
XLA Ops:
  1.3 21.5 %shard_map.131 = (f32[3,256,128]{2,1,0:T(8,128)S(1)}, f32[4,128]{1,0:T(4,128)S(1)}) custom-call(f32[3,256,128]{2,1,0:T(8,128)} %bitcast.13, f32[3,256,128]{2,1,0:T(8,128)} %bitcast.14, f32[3,256,128]{2,1,0:T(8,128)} %bitcast.15, f32[256,128]{1,0:T(8,128)} %bitcast.16, f32[32,128]{1,0:T(8,128)} %bitcast.19, f32[32,128]{1,0:T(8,128)} %bitcast.20, ...), custom_call_target="tpu_custom_call" | custom-call | tf_op jit(solution)/shard_map/pallas_call | solution.py:599
  22.8 0.8 %shard_map.132 = (f32[3,256,128]{2,1,0:T(8,128)}, f32[4,128]{1,0:T(4,128)}) custom-call(f32[3,256,128]{2,1,0:T(8,128)S(1)} %get-tuple-element.6.v_in, f32[4,128]{1,0:T(4,128)S(1)} %get-tuple-element.7.load_in), custom_call_target="tpu_custom_call" | custom-call | tf_op jit(solution)/shard_map/pallas_call | solution.py:623

commit v2 on v1

--- a/solution.py
+++ b/solution.py
@@ -98,12 +98,24 @@
     def blk_peer(offset):
         return {"blk": lax.rem(b + offset, n_blk), "road": r}
 
-    blk_offsets = range(1, n_blk) if in_kernel_sum else sorted({1, n_blk - 1})
+    def blk_place(t):
+        return {"blk": t, "road": r}
+
+    def greet(t, _):
+        pl.semaphore_signal(barrier, inc=1, device_id=blk_place(t), device_id_type=MESH)
+        return 0
+
     barrier = pltpu.get_barrier_semaphore()
-    for offset in reversed(blk_offsets):
-        pl.semaphore_signal(barrier, inc=1, device_id=blk_peer(offset), device_id_type=MESH)
     for offset in range(1, n_road):
         pl.semaphore_signal(barrier, inc=1, device_id=road_peer(offset), device_id_type=MESH)
+    if in_kernel_sum:
+        lax.fori_loop(b - (b + n_blk - 1) // n_blk, b, greet, 0)
+        lax.fori_loop(b + 1, n_blk, greet, 0)
+        greeted = b + 1 - b // (n_blk - 1)
+    else:
+        for offset in sorted({1, n_blk - 1}):
+            greet(lax.rem(b + offset, n_blk), 0)
+        greeted = len({1, n_blk - 1})
 
     def fill_faces(step, source):
         for c in range(3):
@@ -157,18 +169,19 @@
         pltpu.make_async_copy(own[a], facet_all.at[a * n_road + r], own_sems.at[a]) for a in range(4)
     ]
     if in_kernel_sum:
-        tiles_all, loads_all, reduced, blk_recv, tile_sems, road_sems, blk_sems = reduction
+        tiles_all, loads_all, reduced, blk_recv, tile_sems, road_sems, blk_sems, late_sem = reduction
         own_copies.append(pltpu.make_async_copy(tiles_in, tiles_all.at[r], own_sems.at[4]))
     for copy in own_copies:
         copy.start()
-    for copy in loads_in[:2]:
-        copy.wait()
-    fill_faces(0, disp)
-
-    pl.semaphore_wait(barrier, len(blk_offsets) + n_road - 1)
-    halos0 = halo_copies(0)
-    for copy in halos0[:2]:
-        copy.start()
+    pl.semaphore_wait(barrier, greeted + n_road - 1)
+    if in_kernel_sum:
+
+        def tell(t, _):
+            pl.semaphore_signal(late_sem, inc=1, device_id=blk_place(t), device_id_type=MESH)
+            return 0
+
+        lax.fori_loop(0, b, tell, 0)
+
     facet_copies = []
     for a in range(4):
         for offset in range(1, n_road):
@@ -182,8 +195,12 @@
             )
             copy.start()
             facet_copies.append(copy)
-    for copy in halos0[2:]:
-        copy.start()
+    for copy in loads_in[:2]:
+        copy.wait()
+    fill_faces(0, disp)
+    halos0 = halo_copies(0)
+    for i in (0, 2, 3):
+        halos0[i].start()
     tile_copies = []
     if in_kernel_sum:
         for offset in range(1, n_road):
@@ -231,7 +248,7 @@
         def body(i, above):
             return tuple(inside(source, layers - 1 - i, above, False))
 
-        above = lax.fori_loop(0, layers - 1, body, nothing, unroll=3)
+        above = lax.fori_loop(0, layers - 1, body, nothing, unroll=5)
         inside(source, 0, above, True)
 
     def fill_rim(step):
@@ -308,7 +325,7 @@
         return look(lines, slots[group_at(g), :])
 
     def press(g, u, h, sx, sy, ks):
-        live = slot_index + g * (SUB * LANES) < count[0, 0]
+        live = slot_index + g * (SUB * LANES) < count[0]
         return jnp.where(live, ks * jnp.maximum(h + sx * u[0] + sy * u[1] - u[2], 0.0), 0.0)
 
     def wide(ref_row, height_of, dtype):
@@ -378,15 +395,22 @@
             picked[c, group_at(g), :] = x
         return 0
 
-    lax.fori_loop(0, groups, pick_first, 0, unroll=2)
+    lax.fori_loop(0, groups, pick_first, 0, unroll=8)
 
     def fill_scale(k, _):
         at = layer_rows(k)
         scale[at, :] = time_step / mass[at, :]
         return 0
 
-    lax.fori_loop(0, layers, fill_scale, 0, unroll=2)
-
+    lax.fori_loop(0, layers, fill_scale, 0, unroll=8)
+
+    if in_kernel_sum:
+
+        @pl.when(b < n_blk - 1)
+        def _():
+            pl.semaphore_wait(late_sem, n_blk - 1 - b)
+
+    halos0[1].start()
     for copy in loads_in[5:] + own_copies + facet_copies:
         copy.wait()
     for j in range(tiles_need):
@@ -405,8 +429,8 @@
         normals[0, at, :] = press(g, [picked[c, at, :] for c in range(3)], *values)
         return 0
 
-    lax.fori_loop(0, groups, first_press, 0, unroll=2)
-    add_outer(lax.fori_loop(0, groups, functools.partial(scatter_force, 0), no_push, unroll=2))
+    lax.fori_loop(0, groups, first_press, 0, unroll=8)
+    add_outer(lax.fori_loop(0, groups, functools.partial(scatter_force, 0), no_push, unroll=8))
 
     def advance(k, _):
         at = layer_rows(k)
@@ -426,8 +450,8 @@
         normals[1, at, :] = press(g, pick(u1, g), *[facet_vals[a, at, :] for a in range(4)])
         return 0
 
-    lax.fori_loop(0, groups, second_press, 0, unroll=2)
-    loads = lax.fori_loop(0, groups, scatter_load, jnp.zeros((2 * n_rows, LANES), jnp.float32), unroll=2)
+    lax.fori_loop(0, groups, second_press, 0, unroll=8)
+    loads = lax.fori_loop(0, groups, scatter_load, jnp.zeros((2 * n_rows, LANES), jnp.float32), unroll=8)
     loads = loads[:n_rows] + loads[n_rows:]
 
     if in_kernel_sum:
@@ -451,7 +475,7 @@
             total = total + jnp.where(row == tiles[0, j // half] * half + j % half, loads[j : j + 1, :], 0.0)
         load_out[...] = total
 
-    lax.fori_loop(0, layers - 1, advance, 0, unroll=3)
+    lax.fori_loop(0, layers - 1, advance, 0, unroll=5)
     fill_faces(1, u1)
     halos1 = halo_copies(1)
     for copy in halos1:
@@ -485,7 +509,7 @@
             blk_copies.append(copy)
 
     interior(u1)
-    add_outer(lax.fori_loop(0, groups, functools.partial(scatter_force, 1), no_push, unroll=2))
+    add_outer(lax.fori_loop(0, groups, functools.partial(scatter_force, 1), no_push, unroll=8))
     for copy in halos1:
         copy.wait()
     fill_rim(1)
@@ -496,7 +520,7 @@
             v_out[c, at, :] = v1[c, at, :] + scale[at, :] * (force[c, at, :] + rim_force(k, c))
         return 0
 
-    lax.fori_loop(0, layers, finish, 0, unroll=2)
+    lax.fori_loop(0, layers, finish, 0, unroll=8)
 
     if in_kernel_sum:
         for copy in blk_copies:
@@ -557,7 +581,7 @@
         pltpu.VMEM((pair_rows, LANES), jnp.int32),
         pltpu.VMEM((pair_rows, LANES), jnp.int32),
         pltpu.SMEM((1, tiles_need), jnp.int32),
-        pltpu.SMEM((1, 1), jnp.int32),
+        pltpu.SMEM((1,), jnp.int32),
         pltpu.SemaphoreType.DMA((8,)),
         pltpu.SemaphoreType.DMA((5,)),
         pltpu.VMEM((3, pair_rows, LANES), f32),
@@ -592,6 +616,7 @@
             pltpu.SemaphoreType.DMA((2, n_road - 1)),
             pltpu.SemaphoreType.DMA((2, n_road - 1)),
             pltpu.SemaphoreType.DMA((2, n_blk - 1)),
+            pltpu.SemaphoreType.REGULAR,
         ]
     vmem = pl.BlockSpec(memory_space=pltpu.VMEM)
     hbm = pl.BlockSpec(memory_space=pltpu.HBM)
@@ -618,7 +643,7 @@
         tile_list.reshape(1, tiles_need),
         pair_node.reshape(pair_rows, LANES),
         pair_slot.reshape(pair_rows, LANES),
-        pair_count.reshape(1, 1),
+        pair_count.reshape(1,),
     )
     velocity, load = pl.pallas_call(
         write_out,

time: 23.7 us -> 22.3 us (0.941)
  Pallas kernels: 22.3 us -> 20.8 us
    pallas_call x1, Pallas kernels: 21.5 us -> 20.1 us  [on_device(): pl.pallas_call(functools.partial(kernel, n_blk, n_road, lat, in_kernel_su...]
where the time goes in v2:
time: 22.3 us; the launch traced here: 22.1 us
  Pallas kernels  20.8 us (93%)
  between operations  1.29 us (6%)
    pallas_call x1, Pallas kernels, on_device(): pl.pallas_call(functools.partial(kernel, n_blk, n_road, lat, in_kernel_su...  20.1 us
    pallas_call x1, Pallas kernels, on_device(): pl.pallas_call(write_out, out_shape=(jax.ShapeDtypeStruct(velocity.shape,...  0.77 us

profile of v2, /device:TPU:0, one launch (start us, length us, event | category | flops | bytes accessed | tf_op | source)
XLA Modules:
  0.0 22.1 jit_solution(461278389041290632)
XLA Ops:
  1.3 20.1 %shard_map.131 = (f32[3,256,128]{2,1,0:T(8,128)S(1)}, f32[4,128]{1,0:T(4,128)S(1)}) custom-call(f32[3,256,128]{2,1,0:T(8,128)} %bitcast.15, f32[3,256,128]{2,1,0:T(8,128)} %bitcast.16, f32[3,256,128]{2,1,0:T(8,128)} %bitcast.17, f32[256,128]{1,0:T(8,128)} %bitcast.18, f32[32,128]{1,0:T(8,128)} %bitcast.21, f32[32,128]{1,0:T(8,128)} %bitcast.22, ...), custom_call_target="tpu_custom_call" | custom-call | tf_op jit(solution)/shard_map/pallas_call | solution.py:624
  21.3 0.8 %shard_map.132 = (f32[3,256,128]{2,1,0:T(8,128)}, f32[4,128]{1,0:T(4,128)}) custom-call(f32[3,256,128]{2,1,0:T(8,128)S(1)} %get-tuple-element.6.v_in, f32[4,128]{1,0:T(4,128)S(1)} %get-tuple-element.7.load_in), custom_call_target="tpu_custom_call" | custom-call | tf_op jit(solution)/shard_map/pallas_call | solution.py:648

commit v3 on v2

--- a/solution.py
+++ b/solution.py
@@ -105,13 +105,21 @@
         pl.semaphore_signal(barrier, inc=1, device_id=blk_place(t), device_id_type=MESH)
         return 0
 
+    def place(t, offset):
+        return {"blk": t, "road": lax.rem(r + offset, n_road)}
+
+    def notify(sem, offset, t, _):
+        pl.semaphore_signal(sem, inc=1, device_id=place(t, offset), device_id_type=MESH)
+        return 0
+
     barrier = pltpu.get_barrier_semaphore()
     for offset in range(1, n_road):
         pl.semaphore_signal(barrier, inc=1, device_id=road_peer(offset), device_id_type=MESH)
     if in_kernel_sum:
         lax.fori_loop(b - (b + n_blk - 1) // n_blk, b, greet, 0)
-        lax.fori_loop(b + 1, n_blk, greet, 0)
-        greeted = b + 1 - b // (n_blk - 1)
+        for offset in range(n_road):
+            lax.fori_loop(b + 1, n_blk, functools.partial(notify, barrier, offset), 0)
+        greeted = b * n_road + 1 - b // (n_blk - 1)
     else:
         for offset in sorted({1, n_blk - 1}):
             greet(lax.rem(b + offset, n_blk), 0)
@@ -169,18 +177,13 @@
         pltpu.make_async_copy(own[a], facet_all.at[a * n_road + r], own_sems.at[a]) for a in range(4)
     ]
     if in_kernel_sum:
-        tiles_all, loads_all, reduced, blk_recv, tile_sems, road_sems, blk_sems, late_sem = reduction
-        own_copies.append(pltpu.make_async_copy(tiles_in, tiles_all.at[r], own_sems.at[4]))
+        spread_out, spread_recv, spread_sems, late_sem, far_sem = reduction
     for copy in own_copies:
         copy.start()
     pl.semaphore_wait(barrier, greeted + n_road - 1)
     if in_kernel_sum:
-
-        def tell(t, _):
-            pl.semaphore_signal(late_sem, inc=1, device_id=blk_place(t), device_id_type=MESH)
-            return 0
-
-        lax.fori_loop(0, b, tell, 0)
+        for offset in range(n_road):
+            lax.fori_loop(0, b, functools.partial(notify, far_sem if offset else late_sem, offset), 0)
 
     facet_copies = []
     for a in range(4):
@@ -201,19 +204,13 @@
     halos0 = halo_copies(0)
     for i in (0, 2, 3):
         halos0[i].start()
-    tile_copies = []
-    if in_kernel_sum:
-        for offset in range(1, n_road):
-            copy = pltpu.make_async_remote_copy(
-                src_ref=tiles_in,
-                dst_ref=tiles_all.at[r],
-                send_sem=tile_sems.at[0, offset - 1],
-                recv_sem=tile_sems.at[1, offset - 1],
-                device_id=road_peer(offset),
-                device_id_type=MESH,
-            )
-            copy.start()
-            tile_copies.append(copy)
+    if in_kernel_sum:
+
+        @pl.when(b < n_blk - 1)
+        def _():
+            pl.semaphore_wait(late_sem, n_blk - 1 - b)
+
+    halos0[1].start()
 
     lat_index = lax.broadcasted_iota(jnp.int32, (lat, LANES), 0)
     lane_index = lax.broadcasted_iota(jnp.int32, (lat, LANES), 1)
@@ -404,13 +401,6 @@
 
     lax.fori_loop(0, layers, fill_scale, 0, unroll=8)
 
-    if in_kernel_sum:
-
-        @pl.when(b < n_blk - 1)
-        def _():
-            pl.semaphore_wait(late_sem, n_blk - 1 - b)
-
-    halos0[1].start()
     for copy in loads_in[5:] + own_copies + facet_copies:
         copy.wait()
     for j in range(tiles_need):
@@ -421,16 +411,15 @@
                     a * n_road + row // patch_rows, pl.ds(row % patch_rows, 1), :
                 ]
 
-    def first_press(g, _):
+    def first_contact(g, pushed):
         at = group_at(g)
         values = pick_facet(g)
         for a in range(4):
             facet_vals[a, at, :] = values[a]
         normals[0, at, :] = press(g, [picked[c, at, :] for c in range(3)], *values)
-        return 0
-
-    lax.fori_loop(0, groups, first_press, 0, unroll=8)
-    add_outer(lax.fori_loop(0, groups, functools.partial(scatter_force, 0), no_push, unroll=8))
+        return scatter_force(0, g, pushed)
+
+    add_outer(lax.fori_loop(0, groups, first_contact, no_push, unroll=8))
 
     def advance(k, _):
         at = layer_rows(k)
@@ -445,68 +434,49 @@
     fill_rim(0)
     advance(layers - 1, 0)
 
-    def second_press(g, _):
-        at = group_at(g)
-        normals[1, at, :] = press(g, pick(u1, g), *[facet_vals[a, at, :] for a in range(4)])
-        return 0
-
-    lax.fori_loop(0, groups, second_press, 0, unroll=8)
-    loads = lax.fori_loop(0, groups, scatter_load, jnp.zeros((2 * n_rows, LANES), jnp.float32), unroll=8)
-    loads = loads[:n_rows] + loads[n_rows:]
-
-    if in_kernel_sum:
-        loads_all[r] = loads
-        road_copies = []
-        for offset in range(1, n_road):
-            copy = pltpu.make_async_remote_copy(
-                src_ref=loads_all.at[r],
-                dst_ref=loads_all.at[r],
-                send_sem=road_sems.at[0, offset - 1],
-                recv_sem=road_sems.at[1, offset - 1],
-                device_id=road_peer(offset),
-                device_id_type=MESH,
-            )
-            copy.start()
-            road_copies.append(copy)
-    else:
-        row = lax.broadcasted_iota(jnp.int32, load_out.shape, 0)
-        total = jnp.zeros(load_out.shape, jnp.float32)
-        for j in range(n_rows):
-            total = total + jnp.where(row == tiles[0, j // half] * half + j % half, loads[j : j + 1, :], 0.0)
-        load_out[...] = total
-
     lax.fori_loop(0, layers - 1, advance, 0, unroll=5)
     fill_faces(1, u1)
     halos1 = halo_copies(1)
     for copy in halos1:
         copy.start()
 
-    if in_kernel_sum:
-        for copy in tile_copies + road_copies:
-            copy.wait()
+    def second_contact(g, loads):
+        at = group_at(g)
+        normals[1, at, :] = press(g, pick(u1, g), *[facet_vals[a, at, :] for a in range(4)])
+        return scatter_load(g, loads)
+
+    loads = lax.fori_loop(0, groups, second_contact, jnp.zeros((2 * n_rows, LANES), jnp.float32), unroll=8)
+    loads = loads[:n_rows] + loads[n_rows:]
+
+    spread_rows = n_blk * n_road * load_out.shape[0] if in_kernel_sum else load_out.shape[0]
+    row = lax.broadcasted_iota(jnp.int32, (spread_rows, LANES), 0)
+    total = jnp.zeros((spread_rows, LANES), jnp.float32)
+    for j in range(n_rows):
+        total = total + jnp.where(row == tiles[0, j // half] * half + j % half, loads[j : j + 1, :], 0.0)
+    if in_kernel_sum:
         chunk_rows = load_out.shape[0]
-        row = lax.broadcasted_iota(jnp.int32, (n_blk * chunk_rows, LANES), 0)
-        row = (row // chunk_rows * n_road + r) * chunk_rows + row % chunk_rows
-        total = jnp.zeros((n_blk * chunk_rows, LANES), jnp.float32)
-        for i in range(n_road):
-            first_rows = tiles_all[i] * half
-            for j in range(n_rows):
-                here = first_rows[:, j // half : j // half + 1] + j % half
-                total = total + jnp.where(row == here, loads_all[i, j : j + 1, :], 0.0)
-        for i in range(n_blk):
-            reduced[i] = total[i * chunk_rows : (i + 1) * chunk_rows]
-        blk_copies = []
-        for offset in range(1, n_blk):
+        for i in range(n_blk * n_road):
+            spread_out[i] = total[i * chunk_rows : (i + 1) * chunk_rows]
+
+        @pl.when(b < n_blk - 1)
+        def _():
+            pl.semaphore_wait(far_sem, (n_blk - 1 - b) * (n_road - 1))
+
+        load_copies = []
+        for i in range(1, n_blk * n_road):
+            sector = lax.rem(b + i // n_road, n_blk)
             copy = pltpu.make_async_remote_copy(
-                src_ref=reduced.at[lax.rem(b + offset, n_blk)],
-                dst_ref=blk_recv.at[offset - 1],
-                send_sem=blk_sems.at[0, offset - 1],
-                recv_sem=blk_sems.at[1, offset - 1],
-                device_id=blk_peer(offset),
+                src_ref=spread_out.at[sector * n_road + lax.rem(r + i % n_road, n_road)],
+                dst_ref=spread_recv.at[i - 1],
+                send_sem=spread_sems.at[0, i - 1],
+                recv_sem=spread_sems.at[1, i - 1],
+                device_id=place(sector, i % n_road),
                 device_id_type=MESH,
             )
             copy.start()
-            blk_copies.append(copy)
+            load_copies.append(copy)
+    else:
+        load_out[...] = total
 
     interior(u1)
     add_outer(lax.fori_loop(0, groups, functools.partial(scatter_force, 1), no_push, unroll=8))
@@ -523,11 +493,11 @@
     lax.fori_loop(0, layers, finish, 0, unroll=8)
 
     if in_kernel_sum:
-        for copy in blk_copies:
+        for copy in load_copies:
             copy.wait()
-        total = reduced[b]
-        for i in range(n_blk - 1):
-            total = total + blk_recv[i]
+        total = spread_out[b * n_road + r]
+        for i in range(n_blk * n_road - 1):
+            total = total + spread_recv[i]
         load_out[...] = total
 
 
@@ -583,7 +553,7 @@
         pltpu.SMEM((1, tiles_need), jnp.int32),
         pltpu.SMEM((1,), jnp.int32),
         pltpu.SemaphoreType.DMA((8,)),
-        pltpu.SemaphoreType.DMA((5,)),
+        pltpu.SemaphoreType.DMA((4,)),
         pltpu.VMEM((3, pair_rows, LANES), f32),
         pltpu.VMEM((4, pair_rows, LANES), f32),
         pltpu.VMEM((2, pair_rows, LANES), f32),
@@ -609,13 +579,10 @@
     ]
     if in_kernel_sum:
         scratch += [
-            pltpu.VMEM((n_road, 1, tiles_need), jnp.int32),
-            pltpu.VMEM((n_road, table_rows, LANES), f32),
-            pltpu.VMEM((n_blk,) + load_shape, f32),
-            pltpu.VMEM((n_blk - 1,) + load_shape, f32),
-            pltpu.SemaphoreType.DMA((2, n_road - 1)),
-            pltpu.SemaphoreType.DMA((2, n_road - 1)),
-            pltpu.SemaphoreType.DMA((2, n_blk - 1)),
+            pltpu.VMEM((devices,) + load_shape, f32),
+            pltpu.VMEM((devices - 1,) + load_shape, f32),
+            pltpu.SemaphoreType.DMA((2, devices - 1)),
+            pltpu.SemaphoreType.REGULAR,
             pltpu.SemaphoreType.REGULAR,
         ]
     vmem = pl.BlockSpec(memory_space=pltpu.VMEM)

time: 22.3 us -> 21.6 us (0.969)
  Pallas kernels: 20.8 us -> 20.1 us
    pallas_call x1, Pallas kernels: 20.1 us -> 19.4 us  [on_device(): pl.pallas_call(functools.partial(kernel, n_blk, n_road, lat, in_kernel_su...]
where the time goes in v3:
time: 21.6 us; the launch traced here: 21.4 us
  Pallas kernels  20.1 us (93%)
  between operations  1.29 us (6%)
    pallas_call x1, Pallas kernels, on_device(): pl.pallas_call(functools.partial(kernel, n_blk, n_road, lat, in_kernel_su...  19.4 us
    pallas_call x1, Pallas kernels, on_device(): pl.pallas_call(write_out, out_shape=(jax.ShapeDtypeStruct(velocity.shape,...  0.77 us

profile of v3, /device:TPU:0, one launch (start us, length us, event | category | flops | bytes accessed | tf_op | source)
XLA Modules:
  0.0 21.4 jit_solution(10186671558860227709)
XLA Ops:
  1.3 19.4 %shard_map.131 = (f32[3,256,128]{2,1,0:T(8,128)S(1)}, f32[4,128]{1,0:T(4,128)S(1)}) custom-call(f32[3,256,128]{2,1,0:T(8,128)} %bitcast.15, f32[3,256,128]{2,1,0:T(8,128)} %bitcast.16, f32[3,256,128]{2,1,0:T(8,128)} %bitcast.17, f32[256,128]{1,0:T(8,128)} %bitcast.18, f32[32,128]{1,0:T(8,128)} %bitcast.21, f32[32,128]{1,0:T(8,128)} %bitcast.22, ...), custom_call_target="tpu_custom_call" | custom-call | tf_op jit(solution)/shard_map/pallas_call | solution.py:591
  20.7 0.8 %shard_map.132 = (f32[3,256,128]{2,1,0:T(8,128)}, f32[4,128]{1,0:T(4,128)}) custom-call(f32[3,256,128]{2,1,0:T(8,128)S(1)} %get-tuple-element.6.v_in, f32[4,128]{1,0:T(4,128)S(1)} %get-tuple-element.7.load_in), custom_call_target="tpu_custom_call" | custom-call | tf_op jit(solution)/shard_map/pallas_call | solution.py:615
